TPU v7x, 32 devices: a whole 2x2x4 slice. The times are simulated.
32 devices in a mesh: dp: 16 (over z, y, core), tensor: 2 (over x).
Axes of the slice: x: 2, y: 2, z: 4, core: 2. Of those that a mesh axis runs over, the one named last changes fastest.
Arguments:
- tokens: bfloat16 [6144, 2880], P('dp', 'tensor'), may hold values from -6 to 6
- out_grad: bfloat16 [6144, 2880], P('dp', 'tensor'), may hold values from -6 to 6
- route_probs: bfloat16 [6144, 4], P('dp'), may hold values from 0.099609375 to 1
- expert_ids: int32 [6144, 4], P('dp'), may hold values from 0 to 63, all different within a row; in each aligned block of 384 rows (0 to 383, 384 to 767, ...) at most 36 rows name the same one
- placement_map: int32 [64], replicated, may hold values from 0 to 63, each once
- w_gate: bfloat16 [16, 2880, 2880], P('dp', None, 'tensor'), may hold values from -0.109375 to 0.109375
- w_up: bfloat16 [16, 2880, 2880], P('dp', None, 'tensor'), may hold values from -0.109375 to 0.109375
- w_down: bfloat16 [16, 2880, 2880], P('dp', 'tensor'), may hold values from -0.109375 to 0.109375
Outputs:
- input_grad: bfloat16 [6144, 2880], P('dp', 'tensor')
- gate_grad: bfloat16 [16, 2880, 2880], P('dp', None, 'tensor')
- up_grad: bfloat16 [16, 2880, 2880], P('dp', None, 'tensor')
- down_grad: bfloat16 [16, 2880, 2880], P('dp', 'tensor')
- prob_grad: bfloat16 [6144, 4], P('dp')
Inputs may be any that keep to these rules, and one draw needn't show every extreme that they name: `expert_ids`: each row names 4 different experts. In the rows of one index of dp no expert is named by more than 36 rows, a bound that some block reaches. `placement_map`: A permutation: every value is taken by exactly one expert.
All inputs are finite; a program needn't handle non-finite values.
Results may differ from a plain program's by a relative error of at most 0.011.
Values may be sent and summed in bfloat16 or wider, within the bound.
A program may use at most 128 MiB of HBM per device.

v0:
```python
import jax
import jax.numpy as jnp
from jax import lax
from jax.sharding import PartitionSpec as P

EXP_OWN = 4
SWISH_SLOPE = 1.702


def route_layout(expert_ids, placement_map, owners, capacity):
    tok_rows, top_count = expert_ids.shape
    experts = placement_map.shape[0]
    per_owner = experts // owners
    matches = expert_ids[:, :, None] == jnp.arange(experts, dtype=jnp.int32)[None, None, :]
    code_value = jnp.sum(jnp.where(matches, placement_map[None, None, :], 0), axis=-1).reshape(-1)
    in_wave = code_value % per_owner == 0
    owner_of = code_value // per_owner
    chosen = (
        (owner_of[:, None] == jnp.arange(owners, dtype=jnp.int32)[None, :]) & in_wave[:, None]
    ).astype(jnp.int32)
    before = jnp.cumsum(chosen, axis=0) - chosen
    slot_index = jnp.sum(before * chosen, axis=1)
    target = jnp.where(in_wave, owner_of * capacity + slot_index, owners * capacity)
    slot_route = (
        jnp.full((owners * capacity,), -1, jnp.int32)
        .at[target]
        .set(jnp.arange(tok_rows * top_count, dtype=jnp.int32), mode="drop")
    )
    return (in_wave, target, slot_route)


def build_rows(values, slot_route, row_valid, top_count):
    picked = jnp.take(values, jnp.where(row_valid, slot_route // top_count, 0), axis=0)
    return jnp.where(row_valid[:, None], picked, jnp.zeros_like(picked))


def shards(tokens, out_grad, route_probs, expert_ids, placement_map, w_gate, w_up, w_down):
    owners = lax.axis_size("dp")
    tok_rows, top_count = expert_ids.shape
    capacity = 3 * tok_rows * top_count // (2 * EXP_OWN * owners)
    in_wave, target, slot_route = route_layout(expert_ids, placement_map, owners, capacity)
    row_valid = slot_route >= 0
    safe_route = jnp.where(row_valid, slot_route, 0)
    zero_half = jnp.zeros((), jnp.bfloat16)
    prob_rows = jnp.where(row_valid, route_probs.reshape(-1)[safe_route], zero_half)
    part_width = tokens.shape[1]
    send_x = build_rows(tokens, slot_route, row_valid, top_count).reshape(
        owners, capacity, part_width
    )
    send_d = build_rows(out_grad, slot_route, row_valid, top_count).reshape(
        owners, capacity, part_width
    )
    got_x, got_d, got_p = (
        lax.all_to_all(send_x, "dp", split_axis=0, concat_axis=0, tiled=True),
        lax.all_to_all(send_d, "dp", split_axis=0, concat_axis=0, tiled=True),
        lax.all_to_all(
            prob_rows.reshape(owners, capacity), "dp", split_axis=0, concat_axis=0, tiled=True
        ),
    )
    rows_x, rows_d = (
        lax.all_gather(got_x.reshape(owners * capacity, part_width), "tensor", axis=1, tiled=True),
        lax.all_gather(got_d.reshape(owners * capacity, part_width), "tensor", axis=1, tiled=True),
    )
    prob_column = got_p.reshape(-1).astype(jnp.float32)[:, None]
    gate_w = w_gate[0]
    up_w = w_up[0]
    down_w = w_down[0]
    contract_cols = (((1,), (1,)), ((), ()))
    contract_rows = (((0,), (0,)), ((), ()))
    gate_pre = jnp.dot(rows_x, gate_w, preferred_element_type=jnp.float32)
    up_pre = jnp.dot(rows_x, up_w, preferred_element_type=jnp.float32)
    sig_gate = jax.nn.sigmoid(SWISH_SLOPE * gate_pre)
    active = (gate_pre * sig_gate * (up_pre + 1.0)).astype(jnp.bfloat16)
    down_back = lax.dot_general(rows_d, down_w, contract_cols, preferred_element_type=jnp.float32)
    outputs = jnp.dot(active, down_w, preferred_element_type=jnp.float32)
    slice_sum = jnp.sum(rows_d.astype(jnp.float32) * outputs, axis=1)
    prob_sum = lax.psum(slice_sum, "tensor")
    delta_act = prob_column * down_back
    grad_gate_pre = (
        delta_act
        * (up_pre + 1.0)
        * (sig_gate + SWISH_SLOPE * gate_pre * sig_gate * (1.0 - sig_gate))
    ).astype(jnp.bfloat16)
    grad_up_pre = (delta_act * gate_pre * sig_gate).astype(jnp.bfloat16)
    scaled_grad = (prob_column * rows_d.astype(jnp.float32)).astype(jnp.bfloat16)
    down_grad = lax.dot_general(
        active, scaled_grad, contract_rows, preferred_element_type=jnp.float32
    ).astype(jnp.bfloat16)
    gate_grad = lax.dot_general(
        rows_x, grad_gate_pre, contract_rows, preferred_element_type=jnp.float32
    ).astype(jnp.bfloat16)
    up_grad = lax.dot_general(
        rows_x, grad_up_pre, contract_rows, preferred_element_type=jnp.float32
    ).astype(jnp.bfloat16)
    input_part = lax.dot_general(
        grad_gate_pre, gate_w, contract_cols, preferred_element_type=jnp.float32
    ) + lax.dot_general(grad_up_pre, up_w, contract_cols, preferred_element_type=jnp.float32)
    rounded_part = lax.optimization_barrier(input_part.astype(jnp.bfloat16)).astype(jnp.float32)
    input_rows = lax.psum_scatter(
        rounded_part.astype(jnp.bfloat16), "tensor", scatter_dimension=1, tiled=True
    )
    part_cols = input_rows.shape[1]
    back_rows, back_prob = (
        lax.all_to_all(
            input_rows.reshape(owners, capacity, part_cols),
            "dp",
            split_axis=0,
            concat_axis=0,
            tiled=True,
        ),
        lax.all_to_all(
            prob_sum.astype(jnp.bfloat16).reshape(owners, capacity),
            "dp",
            split_axis=0,
            concat_axis=0,
            tiled=True,
        ),
    )
    back_rows = back_rows.reshape(owners * capacity, part_cols)
    back_prob = back_prob.reshape(-1)
    safe_target = jnp.where(in_wave, target, 0)
    route_rows = jnp.where(in_wave[:, None], jnp.take(back_rows, safe_target, axis=0), zero_half)
    input_grad = jnp.sum(
        route_rows.reshape(tok_rows, top_count, part_cols).astype(jnp.float32), axis=1
    ).astype(jnp.bfloat16)
    prob_grad = jnp.where(in_wave, back_prob[safe_target], zero_half).reshape(tok_rows, top_count)
    return (input_grad, gate_grad[None], up_grad[None], down_grad[None], prob_grad)


def solution(mesh):
    in_specs = (
        P("dp", "tensor"),
        P("dp", "tensor"),
        P("dp", None),
        P("dp", None),
        P(),
        P("dp", None, "tensor"),
        P("dp", None, "tensor"),
        P("dp", "tensor", None),
    )
    out_specs = (
        P("dp", "tensor"),
        P("dp", None, "tensor"),
        P("dp", None, "tensor"),
        P("dp", "tensor", None),
        P("dp", None),
    )
    return jax.shard_map(shards, mesh=mesh, in_specs=in_specs, out_specs=out_specs, check_vma=False)
```

profile of v0, /device:TPU:13, one launch (start us, length us, event | category | flops | bytes accessed | tf_op | source)
XLA Modules:
  0.0 413.7 jit_solution(8770292031321615427)
XLA Ops:
  14.8 6.2 %scatter_custom_fusion = s32[576]{0:T(1024)S(1)} fusion(s32[1536]{0:T(1024)S(1)} %get-tuple-element.22, s32[1536]{0:T(1024)S(1)} %iota.15, s32[]{:T(128)} %constant.82.clone.1), kind=kCustom, calls=%fused_computation.111 | custom fusion | bytes 2308 | tf_op jit(solution)/shard_map/scatter | solution.py:27
  37.5 50.9 %all_to_all.35 = bf16[16,36,1440]{2,1,0:T(8,128)(2,1)} all-to-all(bf16[16,36,1440]{2,1,0:T(8,128)(2,1)S(1)} %reshape.291), channel_id=1, replica_groups=mesh['dp'=16,'tensor'=2] {'dp'}, dimensions={0} | all-to-all | bytes 3317760 | tf_op jit(solution)/shard_map/all_to_all | solution.py:54
  94.9 49.4 %all_to_all.36 = bf16[16,36,1440]{2,1,0:T(8,128)(2,1)} all-to-all(bf16[16,36,1440]{2,1,0:T(8,128)(2,1)S(1)} %reshape.289), channel_id=1, replica_groups=mesh['dp'=16,'tensor'=2] {'dp'}, dimensions={0} | all-to-all | bytes 3317760 | tf_op jit(solution)/shard_map/all_to_all | solution.py:55
  152.6 9.0 %all_to_all.37 = bf16[16,1,36]{2,1,0:T(2,128)(2,1)S(1)} all-to-all(bf16[16,1,36]{2,1,0:T(2,128)(2,1)S(1)} %all_to_all.28), channel_id=1, replica_groups=mesh['dp'=16,'tensor'=2] {'dp'}, dimensions={0} | all-to-all | bytes 2304 | tf_op jit(solution)/shard_map/all_to_all | solution.py:56
  162.2 5.6 %copy.46 = bf16[2,1440,576]{1,0,2:T(2,128)(2,1)S(1)} copy(bf16[2,1440,576]{1,2,0:T(8,128)(2,1)} %all-gather.7.cloned.1.call-done) | data formatting | bytes 6635520 | tf_op jit(solution)/shard_map/all_gather | solution.py:61
  172.0 25.0 %all-gather.5.cloned.1.call-done = bf16[2,1440,576]{1,2,0:T(8,128)(2,1)} async-done(((bf16[1,1440,576]{1,2,0:T(8,128)(2,1)}), bf16[2,1440,576]{1,2,0:T(8,128)(2,1)}) %all-gather.5.cloned.1.call-update) | async-done | bytes 3317776 | tf_op jit(solution)/shard_map/all_gather | solution.py:62
  197.0 5.6 %copy.44 = bf16[2,1440,576]{1,0,2:T(2,128)(2,1)S(1)} copy(bf16[2,1440,576]{1,2,0:T(8,128)(2,1)} %all-gather.5.cloned.1.call-done) | data formatting | bytes 6635520 | tf_op jit(solution)/shard_map/all_gather | solution.py:62
  206.8 11.2 %fusion.5 = f32[576,1440]{1,0:T(8,128)} fusion(bf16[2880,576]{0,1:T(8,128)(2,1)} %reshape.351, bf16[1,2880,1440]{1,2,0:T(8,128)(2,1)} %param.15), kind=kOutput, calls=%fused_computation.14 | convolution fusion | flops 4777574400 | bytes 14929920 | tf_op jit(solution)/shard_map/dot_general | solution.py:70
  218.0 19.8 %fusion.21 = f32[576,1440]{1,0:T(8,128)S(1)} fusion(bf16[2880,576]{0,1:T(8,128)(2,1)S(1)} %copy-done.4, bf16[1,1440,2880]{2,1,0:T(8,128)(2,1)} %param.17, f32[576]{0:T(1024)S(1)} %copy-done.8), kind=kOutput, calls=%fused_computation.30 | convolution fusion | flops 4778403840 | bytes 14932224 | tf_op jit(solution)/shard_map/dot_general | solution.py:74
  237.8 12.5 %multiply_convert_fusion = (bf16[576,1440]{1,0:T(8,128)(2,1)}, bf16[576,1440]{1,0:T(8,128)(2,1)}, bf16[576,1440]{1,0:T(8,128)(2,1)S(1)}) fusion(f32[576,1440]{1,0:T(8,128)} %fusion.5, f32[576,1440]{1,0:T(8,128)S(1)} %fusion.21, bf16[2880,576]{0,1:T(8,128)(2,1)S(1)} %copy-done.1, bf16[1,2880,1440]{1,2,0:T(8,128)(2,1)} %param.16), kind=kOutput, calls=%fused_computation.31 | convolution fusion | flops 4792504320 | bytes 23224320 | tf_op jit(solution)/shard_map/dot_general | solution.py:71
  250.3 9.3 %fusion.3 = f32[576,2880]{1,0:T(8,128)S(1)} fusion(bf16[576,1440]{1,0:T(8,128)(2,1)} %get-tuple-element.30, bf16[1,2880,1440]{1,2,0:T(8,128)(2,1)} %param.15), kind=kOutput, calls=%fused_computation.12 | convolution fusion | flops 4777574400 | bytes 16588800 | tf_op jit(solution)/shard_map/dot_general | solution.py:95
  259.7 9.5 %add_convert_fusion = bf16[576,2880]{1,0:T(8,128)(2,1)S(1)} fusion(f32[576,2880]{1,0:T(8,128)S(1)} %fusion.3, bf16[576,1440]{1,0:T(8,128)(2,1)S(1)} %get-tuple-element.31, bf16[1,2880,1440]{1,2,0:T(8,128)(2,1)} %param.16), kind=kOutput, calls=%fused_computation.28 | convolution fusion | flops 4780892160 | bytes 19906560 | tf_op jit(solution)/shard_map/dot_general | solution.py:97
  273.6 9.5 %fusion.16 = f32[576]{0:T(1024)S(1)} fusion(bf16[2880,576]{0,1:T(8,128)(2,1)} %reshape.349, bf16[576,1440]{1,0:T(8,128)(2,1)} %get-tuple-element.29, bf16[1,1440,2880]{2,1,0:T(8,128)(2,1)} %param.17), kind=kOutput, calls=%fused_computation.27 | convolution fusion | flops 4782550528 | bytes 13273344 | tf_op jit(solution)/shard_map/dot_general | solution.py:75
  288.2 7.3 %all-to-all-start.4 = ((bf16[16,1,36]{2,1,0:T(2,128)(2,1)}), bf16[16,1,36]{2,1,0:T(2,128)(2,1)S(1)}, u32[]{:S(2)}, u32[]{:S(2)}) async-start(bf16[16,1,36]{2,1,0:T(2,128)(2,1)} %all_to_all.29), calls=%async_computation.4 | async-start | bytes 16384 | tf_op jit(solution)/shard_map/all_to_all | solution.py:111
  295.5 10.8 %fusion.2 = bf16[1,2880,1440]{1,2,0:T(8,128)(2,1)} fusion(bf16[2880,576]{0,1:T(8,128)(2,1)S(1)} %copy-done.2, bf16[576,1440]{1,0:T(8,128)(2,1)} %copy-done.10), kind=kOutput, calls=%fused_computation.11 | convolution fusion | flops 4781721600 | bytes 13271040 | tf_op jit(solution)/shard_map/dot_general | solution.py:92
  306.3 16.3 %reduce-scatter.4.cloned.1.call-done = bf16[1440,576]{1,0:T(8,128)(2,1)} async-done(((bf16[2880,576]{1,0:T(8,128)(2,1)}), bf16[1440,576]{1,0:T(8,128)(2,1)}) %reduce-scatter.4.cloned.1.call-update) | async-done | bytes 1658896
  326.8 7.1 %all-to-all-start.3 = ((bf16[16,36,1440]{2,1,0:T(8,128)(2,1)}), bf16[16,36,1440]{2,1,0:T(8,128)(2,1)}, u32[]{:S(2)}, u32[]{:S(2)}) async-start(bf16[16,36,1440]{2,1,0:T(8,128)(2,1)} %reshape.293), calls=%async_computation.3 | async-start | bytes 3932160 | tf_op jit(solution)/shard_map/all_to_all | solution.py:104
  333.9 10.9 %fusion.1 = bf16[1,2880,1440]{1,2,0:T(8,128)(2,1)} fusion(bf16[2880,576]{0,1:T(8,128)(2,1)S(1)} %copy-done.3, bf16[576,1440]{1,0:T(8,128)(2,1)} %get-tuple-element.30), kind=kOutput, calls=%fused_computation.10 | convolution fusion | flops 4781721600 | bytes 13271040 | tf_op jit(solution)/shard_map/dot_general | solution.py:89
  344.9 9.5 %fusion = bf16[1,1440,2880]{2,1,0:T(8,128)(2,1)} fusion(bf16[576,1440]{1,0:T(8,128)(2,1)S(1)} %copy-done.11, bf16[2880,576]{0,1:T(8,128)(2,1)S(1)} %copy-done.5, f32[576]{0:T(1024)S(1)} %copy-done.8), kind=kOutput, calls=%fused_computation.9 | convolution fusion | flops 4786698240 | bytes 13273344 | tf_op jit(solution)/shard_map/dot_general | solution.py:86
  354.5 9.5 %gather_fusion.2 = bf16[1536]{0:T(1024)(128)(2,1)S(1)} fusion(bf16[576]{0:T(1024)(128)(2,1)S(1)} %reshape.295, s32[2048]{0:T(1024)S(1)} %pad_clamp_fusion), kind=kCustom, calls=%fused_computation.4 | custom fusion | bytes 12288 | tf_op jit(solution)/shard_map/gather | solution.py:126
  365.3 13.1 %all-to-all-done.3 = bf16[16,36,1440]{2,1,0:T(8,128)(2,1)} async-done(((bf16[16,36,1440]{2,1,0:T(8,128)(2,1)}), bf16[16,36,1440]{2,1,0:T(8,128)(2,1)}, u32[]{:S(2)}, u32[]{:S(2)}) %all-to-all-start.3) | async-done | bytes 1658912 | tf_op jit(solution)/shard_map/all_to_all | solution.py:104
  381.2 6.2 %gather_fusion.1 = bf16[1536,1440]{1,0:T(8,128)(2,1)} fusion(bf16[576,1440]{1,0:T(8,128)(2,1)S(1)} %reshape.294, s32[2048]{0:T(1024)S(1)} %pad_clamp_fusion), kind=kCustom, calls=%fused_computation.3 | custom fusion | bytes 8853504 | tf_op jit(solution)/shard_map/jit(_take)/gather | solution.py:122
  387.4 8.9 %gather.19 = bf16[384,4,1440]{2,1,0:T(4,128)(2,1)} reshape(bf16[1536,1440]{1,0:T(8,128)(2,1)} %gather_fusion.1) | data formatting | bytes 8847360 | tf_op jit(solution)/shard_map/jit(_take)/gather | solution.py:122
  396.3 9.1 %select_reduce_fusion = bf16[384,1440]{1,0:T(8,128)(2,1)S(1)} fusion(bf16[384,4,1440]{2,1,0:T(4,128)(2,1)} %gather.19, pred[384,4]{1,0:T(8,128)(4,1)S(1)} %copy.39, pred[384,4]{1,0:T(8,128)(4,1)S(1)} %copy.35), kind=kLoop, calls=%fused_computation.29 | loop fusion | flops 6082560 | bytes 5532672 | tf_op jit(solution)/shard_map/reduce_sum | solution.py:123
  (89 shorter events, 67.0 us)
Async XLA Ops:
  7.2 15.5 %copy-start.6 = (bf16[384,1440]{0,1:T(8,128)(2,1)S(1)}, bf16[384,1440]{0,1:T(8,128)(2,1)}, u32[]{:S(2)}) copy-start(bf16[384,1440]{0,1:T(8,128)(2,1)} %param.11) | copy-start | bytes 3317764
  7.2 155.1 %all-gather.7.cloned.1.call-start = ((), (), s32[]{:S(2)}) async-start(), calls=%async_computation.7 | async-start | bytes 5308416 | tf_op jit(solution)/shard_map/all_gather | solution.py:61
  27.5 3.6 copy-start
  92.2 104.8 %all-gather.5.cloned.1.call-start = ((), (), s32[]{:S(2)}) async-start(), calls=%async_computation.6 | async-start | bytes 5308416 | tf_op jit(solution)/shard_map/all_gather | solution.py:62
  144.2 3.9 copy-start.9
  148.1 174.5 %reduce-scatter.4.cloned.1.call-start = ((), (), s32[]{:S(2)}) async-start(), calls=%async_computation.8 | async-start | bytes 5529600
  206.8 11.2 %copy-start.4 = (bf16[2880,576]{0,1:T(8,128)(2,1)S(1)}, bf16[2880,576]{0,1:T(8,128)(2,1)}, u32[]{:S(2)}) copy-start(bf16[2880,576]{0,1:T(8,128)(2,1)} %reshape.349) | copy-start | bytes 9953284
  206.8 11.2 %copy-start.8 = (f32[576]{0:T(1024)S(1)}, f32[576]{0:T(1024)}, u32[]{:S(2)}) copy-start(f32[576]{0:T(1024)} %reshape.296) | copy-start | bytes 6916
  218.0 19.8 %copy-start.1 = (bf16[2880,576]{0,1:T(8,128)(2,1)S(1)}, bf16[2880,576]{0,1:T(8,128)(2,1)}, u32[]{:S(2)}) copy-start(bf16[2880,576]{0,1:T(8,128)(2,1)} %reshape.351) | copy-start | bytes 9953284
  250.3 9.3 %copy-start.10 = (bf16[576,1440]{1,0:T(8,128)(2,1)}, bf16[576,1440]{1,0:T(8,128)(2,1)S(1)}, u32[]{:S(2)}) copy-start(bf16[576,1440]{1,0:T(8,128)(2,1)S(1)} %get-tuple-element.31) | copy-start | bytes 4976644
  272.9 0.7 copy-start.7
  273.6 21.9 %copy-start.2 = (bf16[2880,576]{0,1:T(8,128)(2,1)S(1)}, bf16[2880,576]{0,1:T(8,128)(2,1)}, u32[]{:S(2)}) copy-start(bf16[2880,576]{0,1:T(8,128)(2,1)} %reshape.351) | copy-start | bytes 9953284
  288.2 38.5 %all-to-all-start.4 = ((bf16[16,1,36]{2,1,0:T(2,128)(2,1)}), bf16[16,1,36]{2,1,0:T(2,128)(2,1)S(1)}, u32[]{:S(2)}, u32[]{:S(2)}) async-start(bf16[16,1,36]{2,1,0:T(2,128)(2,1)} %all_to_all.29), calls=%async_computation.4 | async-start | bytes 16384 | tf_op jit(solution)/shard_map/all_to_all | solution.py:111
  326.8 7.1 %copy-start.3 = (bf16[2880,576]{0,1:T(8,128)(2,1)S(1)}, bf16[2880,576]{0,1:T(8,128)(2,1)}, u32[]{:S(2)}) copy-start(bf16[2880,576]{0,1:T(8,128)(2,1)} %reshape.351) | copy-start | bytes 9953284
  326.8 51.7 %all-to-all-start.3 = ((bf16[16,36,1440]{2,1,0:T(8,128)(2,1)}), bf16[16,36,1440]{2,1,0:T(8,128)(2,1)}, u32[]{:S(2)}, u32[]{:S(2)}) async-start(bf16[16,36,1440]{2,1,0:T(8,128)(2,1)} %reshape.293), calls=%async_computation.3 | async-start | bytes 3932160 | tf_op jit(solution)/shard_map/all_to_all | solution.py:104
  333.9 11.0 %copy-start.5 = (bf16[2880,576]{0,1:T(8,128)(2,1)S(1)}, bf16[2880,576]{0,1:T(8,128)(2,1)}, u32[]{:S(2)}) copy-start(bf16[2880,576]{0,1:T(8,128)(2,1)} %reshape.349) | copy-start | bytes 9953284
  333.9 11.0 %copy-start.11 = (bf16[576,1440]{1,0:T(8,128)(2,1)S(1)}, bf16[576,1440]{1,0:T(8,128)(2,1)}, u32[]{:S(2)}) copy-start(bf16[576,1440]{1,0:T(8,128)(2,1)} %get-tuple-element.29) | copy-start | bytes 4976644
Sparse Core Ops, SparseCore 0:
  92.3 48.7 all-gather.6
  148.2 48.7 all-gather.4
  273.1 49.4 reduce-scatter.3
where the time goes:
time: 421 us; the launch traced here: 414 us
  blocking collectives  114 us (27%)
  matrix products  103 us (24%)
  local copies, waits for them, and re-layouts  93.4 us (22%)
  waiting for transfers between devices  54.4 us (13%)
  other arithmetic  20.1 us (5%)
  starting transfers between devices  14.5 us (3%)
  between operations  14.5 us (3%)
    all_to_all x1, blocking collectives, shards(): lax.all_to_all(send_x, 'dp', split_axis=0, concat_axis=0, tiled=True)  50.9 us
    all_to_all x1, blocking collectives, shards(): lax.all_to_all(send_d, 'dp', split_axis=0, concat_axis=0, tiled=True)  49.4 us
    all_gather x1, waiting for transfers between devices, shards(): lax.all_gather(got_d.reshape(owners * capacity, part_width), 'tensor', ax...  25 us
    dot_general x1, matrix products, shards(): lax.dot_general(rows_d, down_w, contract_cols, preferred_element_type=jnp...  19.8 us
    unnamed x32, local copies, waits for them, and re-layouts  19.4 us
    unnamed x4, waiting for transfers between devices  16.3 us
    gather x2, local copies, waits for them, and re-layouts, shards(): jnp.take(back_rows, safe_target, axis=0)  15.2 us
    all_to_all x1, waiting for transfers between devices, shards(): lax.all_to_all(input_rows.reshape(owners, capacity, part_cols), 'dp', spl...  13.1 us
  transfers between devices with their start and end apart: 5, of which 3 were waited for; matrix products, arithmetic and copies ran while one was open for 19% of the time, Pallas kernels for 0%

commit v1 on v0

--- a/solution.py
+++ b/solution.py
@@ -5,6 +5,11 @@
 
 EXP_OWN = 4
 SWISH_SLOPE = 1.702
+
+
+def gathered_along(x, mesh_axis, dim):
+    blocks = lax.all_gather(x, mesh_axis)
+    return jnp.concatenate(blocks, axis=dim)
 
 
 def route_layout(expert_ids, placement_map, owners, capacity):
@@ -59,7 +64,7 @@
     )
     rows_x, rows_d = (
         lax.all_gather(got_x.reshape(owners * capacity, part_width), "tensor", axis=1, tiled=True),
-        lax.all_gather(got_d.reshape(owners * capacity, part_width), "tensor", axis=1, tiled=True),
+        gathered_along(got_d.reshape(owners * capacity, part_width), "tensor", 1),
     )
     prob_column = got_p.reshape(-1).astype(jnp.float32)[:, None]
     gate_w = w_gate[0]

time: 421 us -> 421 us (level)
    reshape x1 -> x2, local copies, waits for them, and re-layouts: 3.81 us -> 9.79 us  [gathered_along(): return jnp.concatenate(blocks, axis=dim)]
    all_gather x1 -> x0, local copies, waits for them, and re-layouts: 5.64 us -> none  [shards(): lax.all_gather(got_d.reshape(owners * capacity, part_width), 'tensor', ax...]
    unnamed x32 -> x31, local copies, waits for them, and re-layouts: 19.4 us -> 15.2 us
where the time goes in v1:
time: 421 us; the launch traced here: 414 us
  blocking collectives  114 us (27%)
  matrix products  103 us (24%)
  local copies, waits for them, and re-layouts  93.4 us (22%)
  waiting for transfers between devices  54.4 us (13%)
  other arithmetic  20.1 us (5%)
  starting transfers between devices  14.5 us (3%)
  between operations  14.5 us (3%)
    all_to_all x1, blocking collectives, shards(): lax.all_to_all(send_x, 'dp', split_axis=0, concat_axis=0, tiled=True)  50.9 us
    all_to_all x1, blocking collectives, shards(): lax.all_to_all(send_d, 'dp', split_axis=0, concat_axis=0, tiled=True)  49.4 us
    all_gather x1, waiting for transfers between devices, gathered_along(): blocks = lax.all_gather(x, mesh_axis)  25 us
    dot_general x1, matrix products, shards(): lax.dot_general(rows_d, down_w, contract_cols, preferred_element_type=jnp...  19.8 us
    unnamed x4, waiting for transfers between devices  16.3 us
    unnamed x31, local copies, waits for them, and re-layouts  15.2 us
    gather x2, local copies, waits for them, and re-layouts, shards(): jnp.take(back_rows, safe_target, axis=0)  15.2 us
    all_to_all x1, waiting for transfers between devices, shards(): lax.all_to_all(input_rows.reshape(owners, capacity, part_cols), 'dp', spl...  13.1 us
  transfers between devices with their start and end apart: 5, of which 3 were waited for; matrix products, arithmetic and copies ran while one was open for 19% of the time, Pallas kernels for 0%

profile of v1, /device:TPU:13, one launch (start us, length us, event | category | flops | bytes accessed | tf_op | source)
XLA Modules:
  0.0 413.7 jit_solution(8770292031321615427)
XLA Ops:
  14.8 6.2 %scatter_custom_fusion = s32[576]{0:T(1024)S(1)} fusion(s32[1536]{0:T(1024)S(1)} %get-tuple-element.22, s32[1536]{0:T(1024)S(1)} %iota.15, s32[]{:T(128)} %constant.82.clone.1), kind=kCustom, calls=%fused_computation.111 | custom fusion | bytes 2308 | tf_op jit(solution)/shard_map/scatter | solution.py:32
  37.5 50.9 %all_to_all.35 = bf16[16,36,1440]{2,1,0:T(8,128)(2,1)} all-to-all(bf16[16,36,1440]{2,1,0:T(8,128)(2,1)S(1)} %reshape.295), channel_id=1, replica_groups=mesh['dp'=16,'tensor'=2] {'dp'}, dimensions={0} | all-to-all | bytes 3317760 | tf_op jit(solution)/shard_map/all_to_all | solution.py:59
  94.9 49.4 %all_to_all.36 = bf16[16,36,1440]{2,1,0:T(8,128)(2,1)} all-to-all(bf16[16,36,1440]{2,1,0:T(8,128)(2,1)S(1)} %reshape.292), channel_id=1, replica_groups=mesh['dp'=16,'tensor'=2] {'dp'}, dimensions={0} | all-to-all | bytes 3317760 | tf_op jit(solution)/shard_map/all_to_all | solution.py:60
  152.6 9.0 %all_to_all.37 = bf16[16,1,36]{2,1,0:T(2,128)(2,1)S(1)} all-to-all(bf16[16,1,36]{2,1,0:T(2,128)(2,1)S(1)} %all_to_all.28), channel_id=1, replica_groups=mesh['dp'=16,'tensor'=2] {'dp'}, dimensions={0} | all-to-all | bytes 2304 | tf_op jit(solution)/shard_map/all_to_all | solution.py:61
  162.2 5.6 %copy.46 = bf16[2,1440,576]{1,0,2:T(2,128)(2,1)S(1)} copy(bf16[2,1440,576]{1,2,0:T(8,128)(2,1)} %all-gather.6.cloned.1.call-done) | data formatting | bytes 6635520 | tf_op jit(solution)/shard_map/all_gather | solution.py:66
  172.0 25.0 %all-gather.4.cloned.1.call-done = bf16[2,576,1440]{2,1,0:T(8,128)(2,1)} async-done(((bf16[1,576,1440]{2,1,0:T(8,128)(2,1)}), bf16[2,576,1440]{2,1,0:T(8,128)(2,1)}) %all-gather.4.cloned.1.call-update) | async-done | bytes 3317776 | tf_op jit(solution)/shard_map/all_gather | solution.py:11
  197.0 5.6 %copy.44 = bf16[576,2,1440]{2,1,0:T(2,128)(2,1)S(1)} copy(bf16[576,2,1440]{2,0,1:T(8,128)(2,1)} %bitcast.71) | data formatting | bytes 6635520 | tf_op jit(solution)/shard_map/reshape | solution.py:12
  206.8 11.2 %fusion.5 = f32[576,1440]{1,0:T(8,128)} fusion(bf16[2880,576]{0,1:T(8,128)(2,1)} %reshape.353, bf16[1,2880,1440]{1,2,0:T(8,128)(2,1)} %param.15), kind=kOutput, calls=%fused_computation.14 | convolution fusion | flops 4777574400 | bytes 14929920 | tf_op jit(solution)/shard_map/dot_general | solution.py:75
  218.0 19.8 %fusion.21 = f32[576,1440]{1,0:T(8,128)S(1)} fusion(bf16[576,2880]{1,0:T(8,128)(2,1)S(1)} %copy-done.4, bf16[1,1440,2880]{2,1,0:T(8,128)(2,1)} %param.17, f32[576]{0:T(1024)S(1)} %copy-done.8), kind=kOutput, calls=%fused_computation.30 | convolution fusion | flops 4778403840 | bytes 14932224 | tf_op jit(solution)/shard_map/dot_general | solution.py:79
  237.8 12.5 %multiply_convert_fusion = (bf16[576,1440]{1,0:T(8,128)(2,1)}, bf16[576,1440]{1,0:T(8,128)(2,1)}, bf16[576,1440]{1,0:T(8,128)(2,1)S(1)}) fusion(f32[576,1440]{1,0:T(8,128)} %fusion.5, f32[576,1440]{1,0:T(8,128)S(1)} %fusion.21, bf16[2880,576]{0,1:T(8,128)(2,1)S(1)} %copy-done.1, bf16[1,2880,1440]{1,2,0:T(8,128)(2,1)} %param.16), kind=kOutput, calls=%fused_computation.31 | convolution fusion | flops 4792504320 | bytes 23224320 | tf_op jit(solution)/shard_map/dot_general | solution.py:76
  250.3 9.3 %fusion.3 = f32[576,2880]{1,0:T(8,128)S(1)} fusion(bf16[576,1440]{1,0:T(8,128)(2,1)} %get-tuple-element.30, bf16[1,2880,1440]{1,2,0:T(8,128)(2,1)} %param.15), kind=kOutput, calls=%fused_computation.12 | convolution fusion | flops 4777574400 | bytes 16588800 | tf_op jit(solution)/shard_map/dot_general | solution.py:100
  259.7 9.5 %add_convert_fusion = bf16[576,2880]{1,0:T(8,128)(2,1)S(1)} fusion(f32[576,2880]{1,0:T(8,128)S(1)} %fusion.3, bf16[576,1440]{1,0:T(8,128)(2,1)S(1)} %get-tuple-element.31, bf16[1,2880,1440]{1,2,0:T(8,128)(2,1)} %param.16), kind=kOutput, calls=%fused_computation.28 | convolution fusion | flops 4780892160 | bytes 19906560 | tf_op jit(solution)/shard_map/dot_general | solution.py:102
  273.6 9.5 %fusion.16 = f32[576]{0:T(1024)S(1)} fusion(bf16[576,2880]{1,0:T(8,128)(2,1)} %reshape.294, bf16[576,1440]{1,0:T(8,128)(2,1)} %get-tuple-element.29, bf16[1,1440,2880]{2,1,0:T(8,128)(2,1)} %param.17), kind=kOutput, calls=%fused_computation.27 | convolution fusion | flops 4782550528 | bytes 13273344 | tf_op jit(solution)/shard_map/dot_general | solution.py:80
  288.2 7.3 %all-to-all-start.4 = ((bf16[16,1,36]{2,1,0:T(2,128)(2,1)}), bf16[16,1,36]{2,1,0:T(2,128)(2,1)S(1)}, u32[]{:S(2)}, u32[]{:S(2)}) async-start(bf16[16,1,36]{2,1,0:T(2,128)(2,1)} %all_to_all.29), calls=%async_computation.4 | async-start | bytes 16384 | tf_op jit(solution)/shard_map/all_to_all | solution.py:116
  295.5 10.8 %fusion.2 = bf16[1,2880,1440]{1,2,0:T(8,128)(2,1)} fusion(bf16[2880,576]{0,1:T(8,128)(2,1)S(1)} %copy-done.2, bf16[576,1440]{1,0:T(8,128)(2,1)} %copy-done.10), kind=kOutput, calls=%fused_computation.11 | convolution fusion | flops 4781721600 | bytes 13271040 | tf_op jit(solution)/shard_map/dot_general | solution.py:97
  306.3 16.3 %reduce-scatter.4.cloned.1.call-done = bf16[1440,576]{1,0:T(8,128)(2,1)} async-done(((bf16[2880,576]{1,0:T(8,128)(2,1)}), bf16[1440,576]{1,0:T(8,128)(2,1)}) %reduce-scatter.4.cloned.1.call-update) | async-done | bytes 1658896
  326.8 7.1 %all-to-all-start.3 = ((bf16[16,36,1440]{2,1,0:T(8,128)(2,1)}), bf16[16,36,1440]{2,1,0:T(8,128)(2,1)}, u32[]{:S(2)}, u32[]{:S(2)}) async-start(bf16[16,36,1440]{2,1,0:T(8,128)(2,1)} %reshape.297), calls=%async_computation.3 | async-start | bytes 3932160 | tf_op jit(solution)/shard_map/all_to_all | solution.py:109
  333.9 10.9 %fusion.1 = bf16[1,2880,1440]{1,2,0:T(8,128)(2,1)} fusion(bf16[2880,576]{0,1:T(8,128)(2,1)S(1)} %copy-done.3, bf16[576,1440]{1,0:T(8,128)(2,1)} %get-tuple-element.30), kind=kOutput, calls=%fused_computation.10 | convolution fusion | flops 4781721600 | bytes 13271040 | tf_op jit(solution)/shard_map/dot_general | solution.py:94
  344.9 9.5 %fusion = bf16[1,1440,2880]{2,1,0:T(8,128)(2,1)} fusion(bf16[576,1440]{1,0:T(8,128)(2,1)S(1)} %copy-done.11, bf16[576,2880]{1,0:T(8,128)(2,1)S(1)} %copy-done.5, f32[576]{0:T(1024)S(1)} %copy-done.8), kind=kOutput, calls=%fused_computation.9 | convolution fusion | flops 4786698240 | bytes 13273344 | tf_op jit(solution)/shard_map/dot_general | solution.py:91
  354.5 9.5 %gather_fusion.2 = bf16[1536]{0:T(1024)(128)(2,1)S(1)} fusion(bf16[576]{0:T(1024)(128)(2,1)S(1)} %reshape.299, s32[2048]{0:T(1024)S(1)} %pad_clamp_fusion), kind=kCustom, calls=%fused_computation.4 | custom fusion | bytes 12288 | tf_op jit(solution)/shard_map/gather | solution.py:131
  365.3 13.1 %all-to-all-done.3 = bf16[16,36,1440]{2,1,0:T(8,128)(2,1)} async-done(((bf16[16,36,1440]{2,1,0:T(8,128)(2,1)}), bf16[16,36,1440]{2,1,0:T(8,128)(2,1)}, u32[]{:S(2)}, u32[]{:S(2)}) %all-to-all-start.3) | async-done | bytes 1658912 | tf_op jit(solution)/shard_map/all_to_all | solution.py:109
  381.2 6.2 %gather_fusion.1 = bf16[1536,1440]{1,0:T(8,128)(2,1)} fusion(bf16[576,1440]{1,0:T(8,128)(2,1)S(1)} %reshape.298, s32[2048]{0:T(1024)S(1)} %pad_clamp_fusion), kind=kCustom, calls=%fused_computation.3 | custom fusion | bytes 8853504 | tf_op jit(solution)/shard_map/jit(_take)/gather | solution.py:127
  387.4 8.9 %gather.19 = bf16[384,4,1440]{2,1,0:T(4,128)(2,1)} reshape(bf16[1536,1440]{1,0:T(8,128)(2,1)} %gather_fusion.1) | data formatting | bytes 8847360 | tf_op jit(solution)/shard_map/jit(_take)/gather | solution.py:127
  396.3 9.1 %select_reduce_fusion = bf16[384,1440]{1,0:T(8,128)(2,1)S(1)} fusion(bf16[384,4,1440]{2,1,0:T(4,128)(2,1)} %gather.19, pred[384,4]{1,0:T(8,128)(4,1)S(1)} %copy.39, pred[384,4]{1,0:T(8,128)(4,1)S(1)} %copy.35), kind=kLoop, calls=%fused_computation.29 | loop fusion | flops 6082560 | bytes 5532672 | tf_op jit(solution)/shard_map/reduce_sum | solution.py:128
  (89 shorter events, 67.0 us)
Async XLA Ops:
  7.2 15.5 %copy-start.6 = (bf16[384,1440]{0,1:T(8,128)(2,1)S(1)}, bf16[384,1440]{0,1:T(8,128)(2,1)}, u32[]{:S(2)}) copy-start(bf16[384,1440]{0,1:T(8,128)(2,1)} %param.11) | copy-start | bytes 3317764
  7.2 155.1 %all-gather.6.cloned.1.call-start = ((), (), s32[]{:S(2)}) async-start(), calls=%async_computation.7 | async-start | bytes 5308416 | tf_op jit(solution)/shard_map/all_gather | solution.py:66
  27.5 3.6 copy-start
  92.2 104.8 %all-gather.4.cloned.1.call-start = ((), (), s32[]{:S(2)}) async-start(), calls=%async_computation.6 | async-start | bytes 5308416 | tf_op jit(solution)/shard_map/all_gather | solution.py:11
  144.2 3.9 copy-start.9
  148.1 174.5 %reduce-scatter.4.cloned.1.call-start = ((), (), s32[]{:S(2)}) async-start(), calls=%async_computation.8 | async-start | bytes 5529600
  206.8 11.2 %copy-start.4 = (bf16[576,2880]{1,0:T(8,128)(2,1)S(1)}, bf16[576,2880]{1,0:T(8,128)(2,1)}, u32[]{:S(2)}) copy-start(bf16[576,2880]{1,0:T(8,128)(2,1)} %reshape.294) | copy-start | bytes 9953284
  206.8 11.2 %copy-start.8 = (f32[576]{0:T(1024)S(1)}, f32[576]{0:T(1024)}, u32[]{:S(2)}) copy-start(f32[576]{0:T(1024)} %reshape.300) | copy-start | bytes 6916
  218.0 19.8 %copy-start.1 = (bf16[2880,576]{0,1:T(8,128)(2,1)S(1)}, bf16[2880,576]{0,1:T(8,128)(2,1)}, u32[]{:S(2)}) copy-start(bf16[2880,576]{0,1:T(8,128)(2,1)} %reshape.353) | copy-start | bytes 9953284
  250.3 9.3 %copy-start.10 = (bf16[576,1440]{1,0:T(8,128)(2,1)}, bf16[576,1440]{1,0:T(8,128)(2,1)S(1)}, u32[]{:S(2)}) copy-start(bf16[576,1440]{1,0:T(8,128)(2,1)S(1)} %get-tuple-element.31) | copy-start | bytes 4976644
  272.9 0.7 copy-start.7
  273.6 21.9 %copy-start.2 = (bf16[2880,576]{0,1:T(8,128)(2,1)S(1)}, bf16[2880,576]{0,1:T(8,128)(2,1)}, u32[]{:S(2)}) copy-start(bf16[2880,576]{0,1:T(8,128)(2,1)} %reshape.353) | copy-start | bytes 9953284
  288.2 38.5 %all-to-all-start.4 = ((bf16[16,1,36]{2,1,0:T(2,128)(2,1)}), bf16[16,1,36]{2,1,0:T(2,128)(2,1)S(1)}, u32[]{:S(2)}, u32[]{:S(2)}) async-start(bf16[16,1,36]{2,1,0:T(2,128)(2,1)} %all_to_all.29), calls=%async_computation.4 | async-start | bytes 16384 | tf_op jit(solution)/shard_map/all_to_all | solution.py:116
  326.8 7.1 %copy-start.3 = (bf16[2880,576]{0,1:T(8,128)(2,1)S(1)}, bf16[2880,576]{0,1:T(8,128)(2,1)}, u32[]{:S(2)}) copy-start(bf16[2880,576]{0,1:T(8,128)(2,1)} %reshape.353) | copy-start | bytes 9953284
  326.8 51.7 %all-to-all-start.3 = ((bf16[16,36,1440]{2,1,0:T(8,128)(2,1)}), bf16[16,36,1440]{2,1,0:T(8,128)(2,1)}, u32[]{:S(2)}, u32[]{:S(2)}) async-start(bf16[16,36,1440]{2,1,0:T(8,128)(2,1)} %reshape.297), calls=%async_computation.3 | async-start | bytes 3932160 | tf_op jit(solution)/shard_map/all_to_all | solution.py:109
  333.9 11.0 %copy-start.5 = (bf16[576,2880]{1,0:T(8,128)(2,1)S(1)}, bf16[576,2880]{1,0:T(8,128)(2,1)}, u32[]{:S(2)}) copy-start(bf16[576,2880]{1,0:T(8,128)(2,1)} %reshape.294) | copy-start | bytes 9953284
  333.9 11.0 %copy-start.11 = (bf16[576,1440]{1,0:T(8,128)(2,1)S(1)}, bf16[576,1440]{1,0:T(8,128)(2,1)}, u32[]{:S(2)}) copy-start(bf16[576,1440]{1,0:T(8,128)(2,1)} %get-tuple-element.29) | copy-start | bytes 4976644
Sparse Core Ops, SparseCore 0:
  92.3 48.7 all-gather.5
  148.2 48.7 all-gather.3
  273.1 49.4 reduce-scatter.3
